TPU v7x, 32 devices: a whole 2x2x4 slice. The times are simulated.
32 devices in a mesh: dp: 2 (over core), ctx: 4 (over z), fsdp: 4 (over y, x).
Axes of the slice: x: 2, y: 2, z: 4, core: 2. Of those that a mesh axis runs over, the one named last changes fastest.
Arguments:
- tokens: bfloat16 [8, 2, 1024, 2048], P(('dp', 'fsdp'), None, 'ctx'), may hold values from -6 to 6
- cotangent: bfloat16 [8, 2, 1024, 2048], P(('dp', 'fsdp'), None, 'ctx'), may hold values from -6 to 6
- lengths: int32 [8, 2], P(('dp', 'fsdp')), may hold values from 513 to 1024, as said below
- deal: int32 [8, 2, 8], P(('dp', 'fsdp')), may hold values from 0 to 7, each once within a row
- ln_gain: bfloat16 [2048], P('fsdp'), may hold values from 0.5 to 1.5
- ln_bias: bfloat16 [2048], P('fsdp'), may hold values from -1 to 1
- w_qkv: bfloat16 [2048, 6144], P('fsdp'), may hold values from -0.125 to 0.125
- b_qkv: bfloat16 [6144], P('fsdp'), may hold values from -1 to 1
- w_out: bfloat16 [2048, 2048], P('fsdp'), may hold values from -3 to 3
- b_out: bfloat16 [2048], P('fsdp'), may hold values from -2.5 to 2.5
- w_up: bfloat16 [2048, 8192], P('fsdp'), may hold values from -0.125 to 0.125
- b_up: bfloat16 [8192], P('fsdp'), may hold values from -1 to 1
- w_down: bfloat16 [8192, 2048], P('fsdp'), may hold values from -0.0625 to 0.0625
- b_down: bfloat16 [2048], P('fsdp'), may hold values from -2.5 to 2.5
Outputs:
- outputs: bfloat16 [8, 2, 1024, 2048], P(('dp', 'fsdp'), None, 'ctx')
- input_grad: bfloat16 [8, 2, 1024, 2048], P(('dp', 'fsdp'), None, 'ctx')
- grad_ln_gain: float32 [2048], P('fsdp')
- grad_ln_bias: float32 [2048], P('fsdp')
- grad_w_qkv: float32 [2048, 6144], P('fsdp')
- grad_b_qkv: float32 [6144], P('fsdp')
- grad_w_out: float32 [2048, 2048], P('fsdp')
- grad_b_out: float32 [2048], P('fsdp')
- grad_w_up: float32 [2048, 8192], P('fsdp')
- grad_b_up: float32 [8192], P('fsdp')
- grad_w_down: float32 [8192, 2048], P('fsdp')
- grad_b_down: float32 [2048], P('fsdp')
Inputs may be any that keep to these rules, and one draw needn't show every extreme that they name: lengths[g, m] tokens fill the first positions of a sequence, the rest is padding; in every draw one sequence is exactly 1024 long and one exactly 513. Each row of deal is a permutation of the 8 blocks of a sequence.
All inputs are finite; a program needn't handle non-finite values.
Results may differ from a plain program's by a relative error of at most 0.02.
Values may be sent and summed in bfloat16 or wider, within the bound.
No kernel may reach another device: no remote copies, remote signals or barrier semaphores. Data moves between devices by JAX's collectives and lax.ppermute only.
A program may use at most 832 MiB of HBM per device.

v0:
```python
import jax
import jax.numpy as jnp
from jax import lax
from jax.sharding import PartitionSpec as P

HEAD_DIM = 64
ROT = 32
EPS = 1e-05
BASE = 10000.0


def contract_rows(left, right):
    return lax.dot_general(
        left, right, (((0,), (0,)), ((), ())), preferred_element_type=jnp.float32
    )


def contract_cols(left, right):
    return lax.dot_general(
        left, right, (((1,), (1,)), ((), ())), preferred_element_type=jnp.float32
    )


def angles_of(positions):
    half = ROT // 2
    freqs = BASE ** (-(jnp.arange(half, dtype=jnp.float32) * 2.0) / ROT)
    angles = positions.astype(jnp.float32)[:, None] * freqs[None, :]
    return (jnp.cos(angles)[:, None, :], jnp.sin(angles)[:, None, :])


def rotate(values, cosine, sine):
    half = ROT // 2
    first = values[..., :half]
    second = values[..., half:ROT]
    return jnp.concatenate(
        [first * cosine - second * sine, second * cosine + first * sine, values[..., ROT:]], axis=-1
    )


def rotate_back(values, cosine, sine):
    half = ROT // 2
    first = values[..., :half]
    second = values[..., half:ROT]
    return jnp.concatenate(
        [first * cosine + second * sine, second * cosine - first * sine, values[..., ROT:]], axis=-1
    )


def layer_step(weights, inputs, upstream, length, deal_row):
    gain, shift, w_qkv, b_qkv, w_out, b_out, w_up, b_up, w_down, b_down = weights
    row_count, width = inputs.shape
    block_rows = row_count // 2
    head_count = width // HEAD_DIM
    scale = HEAD_DIM ** (-0.5)
    place = lax.axis_index("ctx")
    offsets = jnp.arange(block_rows, dtype=jnp.int32)
    own_blocks = lax.dynamic_slice_in_dim(deal_row, 2 * place, 2)
    local_pos = (own_blocks[:, None] * block_rows + offsets[None, :]).reshape(row_count)
    every_pos = (deal_row[:, None] * block_rows + offsets[None, :]).reshape(-1)
    valid = (local_pos < length).astype(jnp.float32)[:, None]
    allowed = (every_pos[None, :] <= local_pos[:, None]) & (every_pos[None, :] < length)
    cosine, sine = angles_of(local_pos)
    inputs_f = inputs.astype(jnp.float32)
    gain_f = gain.astype(jnp.float32)
    centered = inputs_f - jnp.mean(inputs_f, axis=-1, keepdims=True)
    variance = jnp.mean(centered * centered, axis=-1, keepdims=True)
    inv_std = lax.rsqrt(variance + EPS)
    normed = centered * inv_std
    hidden = (normed * gain_f + shift.astype(jnp.float32)).astype(jnp.bfloat16)
    joined = jnp.dot(hidden, w_qkv, preferred_element_type=jnp.float32) + b_qkv.astype(jnp.float32)
    query = (
        rotate(joined[:, :width].reshape(row_count, head_count, HEAD_DIM), cosine, sine)
        .reshape(row_count, width)
        .astype(jnp.bfloat16)
    )
    keyed = (
        rotate(joined[:, width : 2 * width].reshape(row_count, head_count, HEAD_DIM), cosine, sine)
        .reshape(row_count, width)
        .astype(jnp.bfloat16)
    )
    valued = joined[:, 2 * width :].astype(jnp.bfloat16)
    keys_all, values_all = (
        lax.all_gather(keyed, "ctx", axis=0, tiled=True),
        lax.all_gather(valued, "ctx", axis=0, tiled=True),
    )
    total_keys = keys_all.shape[0]
    group = min(8, head_count)
    span = group * HEAD_DIM

    def heads_of(array, start, count):
        return array[:, start : start + span].reshape(count, group, HEAD_DIM)

    def block_scores(start):
        raw = (
            jnp.einsum(
                "qhd,khd->hqk",
                heads_of(query, start, row_count),
                heads_of(keys_all, start, total_keys),
                preferred_element_type=jnp.float32,
            )
            * scale
        )
        return jnp.where(allowed[None], raw, -1e30)

    attended_parts = []
    lse_parts = []
    for start in range(0, width, span):
        masked = block_scores(start)
        highest = jnp.max(masked, axis=-1, keepdims=True)
        expo = jnp.exp(masked - highest)
        total = jnp.sum(expo, axis=-1, keepdims=True)
        weights_low = (expo / total).astype(jnp.bfloat16)
        mixed = jnp.einsum(
            "hqk,khd->qhd",
            weights_low,
            heads_of(values_all, start, total_keys),
            preferred_element_type=jnp.float32,
        )
        attended_parts.append(mixed.reshape(row_count, span))
        lse_parts.append(highest + jnp.log(total))
    attended = jnp.concatenate(attended_parts, axis=1).astype(jnp.bfloat16)
    branch = jnp.dot(attended, w_out, preferred_element_type=jnp.float32) + b_out.astype(
        jnp.float32
    )
    upward = jnp.dot(hidden, w_up, preferred_element_type=jnp.float32) + b_up.astype(jnp.float32)
    activated = jax.nn.gelu(upward, approximate=True).astype(jnp.bfloat16)
    feed = jnp.dot(activated, w_down, preferred_element_type=jnp.float32) + b_down.astype(
        jnp.float32
    )
    result = (valid * (inputs_f + branch + feed)).astype(jnp.bfloat16)
    grad_out = upstream.astype(jnp.float32) * valid
    grad_low = grad_out.astype(jnp.bfloat16)
    row_total = jnp.sum(grad_out, axis=0)
    d_down = contract_rows(activated, grad_low)
    d_wout = contract_rows(attended, grad_low)
    d_act = contract_cols(grad_low, w_down)
    _, gelu_pull = jax.vjp(lambda value: jax.nn.gelu(value, approximate=True), upward)
    d_upward = gelu_pull(d_act)[0].astype(jnp.bfloat16)
    d_wup = contract_rows(hidden, d_upward)
    d_bup = jnp.sum(d_upward.astype(jnp.float32), axis=0)
    d_attended = contract_cols(grad_low, w_out).astype(jnp.bfloat16)
    dq_parts = []
    dk_parts = []
    dv_parts = []
    delta_parts = []
    for index, start in enumerate(range(0, width, span)):
        masked = block_scores(start)
        probs = jnp.where(allowed[None], jnp.exp(masked - lse_parts[index]), 0.0)
        d_heads = heads_of(d_attended, start, row_count)
        d_probs = jnp.einsum(
            "qhd,khd->hqk",
            d_heads,
            heads_of(values_all, start, total_keys),
            preferred_element_type=jnp.float32,
        )
        delta = jnp.sum(probs * d_probs, axis=-1, keepdims=True)
        d_scores = (probs * (d_probs - delta)).astype(jnp.bfloat16)
        d_query = (
            jnp.einsum(
                "hqk,khd->qhd",
                d_scores,
                heads_of(keys_all, start, total_keys),
                preferred_element_type=jnp.float32,
            )
            * scale
        )
        dq_parts.append(d_query.reshape(row_count, span))
        delta_parts.append(delta[:, :, 0].T)
        d_keyed = (
            jnp.einsum(
                "hqk,qhd->khd",
                d_scores,
                heads_of(query, start, row_count),
                preferred_element_type=jnp.float32,
            )
            * scale
        )
        d_valued = jnp.einsum(
            "hqk,qhd->khd", probs.astype(jnp.bfloat16), d_heads, preferred_element_type=jnp.float32
        )
        dk_parts.append(d_keyed.reshape(total_keys, span))
        dv_parts.append(d_valued.reshape(total_keys, span))
    keys_grad_all = jnp.concatenate(dk_parts, axis=1)
    values_grad_all = jnp.concatenate(dv_parts, axis=1)
    keys_grad, values_grad = (
        lax.psum_scatter(
            keys_grad_all.astype(jnp.bfloat16), "ctx", scatter_dimension=0, tiled=True
        ).astype(jnp.float32),
        lax.psum_scatter(
            values_grad_all.astype(jnp.bfloat16), "ctx", scatter_dimension=0, tiled=True
        ).astype(jnp.float32),
    )
    query_grad = rotate_back(
        jnp.concatenate(dq_parts, axis=1).reshape(row_count, head_count, HEAD_DIM), cosine, sine
    ).reshape(row_count, width)
    keyed_grad = rotate_back(
        keys_grad.reshape(row_count, head_count, HEAD_DIM), cosine, sine
    ).reshape(row_count, width)
    d_joined = jnp.concatenate([query_grad, keyed_grad, values_grad], axis=1).astype(jnp.bfloat16)
    d_wqkv = contract_rows(hidden, d_joined)
    d_bqkv = jnp.sum(d_joined.astype(jnp.float32), axis=0)
    d_hidden = contract_cols(d_joined, w_qkv) + contract_cols(d_upward, w_up)
    d_gain = jnp.sum(d_hidden * normed, axis=0)
    d_shift = jnp.sum(d_hidden, axis=0)
    d_norm = d_hidden * gain_f
    d_inputs = inv_std * (
        d_norm
        - jnp.mean(d_norm, axis=-1, keepdims=True)
        - normed * jnp.mean(d_norm * normed, axis=-1, keepdims=True)
    )
    back = (grad_out + d_inputs).astype(jnp.bfloat16)
    return (
        result,
        back,
        (d_gain, d_shift, d_wqkv, d_bqkv, d_wout, row_total, d_wup, d_bup, d_down, row_total),
    )


def body(
    tokens,
    cotangent,
    lengths,
    deal,
    ln_gain,
    ln_bias,
    w_qkv,
    b_qkv,
    w_out,
    b_out,
    w_up,
    b_up,
    w_down,
    b_down,
):
    shards = (ln_gain, ln_bias, w_qkv, b_qkv, w_out, b_out, w_up, b_up, w_down, b_down)
    shard_count = lax.axis_size("fsdp")
    summed = tuple(
        (
            jnp.zeros((piece.shape[0] * shard_count,) + piece.shape[1:], jnp.float32)
            for piece in shards
        )
    )
    results = []
    backs = []
    for micro_index in range(tokens.shape[1]):
        gathered = (
            lax.all_gather(ln_gain, "fsdp", axis=0, tiled=True),
            lax.all_gather(ln_bias, "fsdp", axis=0, tiled=True),
            lax.all_gather(w_qkv, "fsdp", axis=0, tiled=True),
            lax.all_gather(b_qkv, "fsdp", axis=0, tiled=True),
            lax.all_gather(w_out, "fsdp", axis=0, tiled=True),
            lax.all_gather(b_out, "fsdp", axis=0, tiled=True),
            lax.all_gather(w_up, "fsdp", axis=0, tiled=True),
            lax.all_gather(b_up, "fsdp", axis=0, tiled=True),
            lax.all_gather(w_down, "fsdp", axis=0, tiled=True),
            lax.all_gather(b_down, "fsdp", axis=0, tiled=True),
        )
        result, back, local = layer_step(
            gathered,
            tokens[0, micro_index],
            cotangent[0, micro_index],
            lengths[0, micro_index],
            deal[0, micro_index],
        )
        results.append(result)
        backs.append(back)
        summed = tuple((older + newer for older, newer in zip(summed, local)))
    summed = (
        lax.psum_scatter(
            summed[0].astype(jnp.bfloat16), "fsdp", scatter_dimension=0, tiled=True
        ).astype(jnp.float32),
        lax.psum_scatter(
            summed[1].astype(jnp.bfloat16), "fsdp", scatter_dimension=0, tiled=True
        ).astype(jnp.float32),
        lax.psum_scatter(
            summed[2].astype(jnp.bfloat16), "fsdp", scatter_dimension=0, tiled=True
        ).astype(jnp.float32),
        lax.psum_scatter(
            summed[3].astype(jnp.bfloat16), "fsdp", scatter_dimension=0, tiled=True
        ).astype(jnp.float32),
        lax.psum_scatter(
            summed[4].astype(jnp.bfloat16), "fsdp", scatter_dimension=0, tiled=True
        ).astype(jnp.float32),
        lax.psum_scatter(
            summed[5].astype(jnp.bfloat16), "fsdp", scatter_dimension=0, tiled=True
        ).astype(jnp.float32),
        lax.psum_scatter(
            summed[6].astype(jnp.bfloat16), "fsdp", scatter_dimension=0, tiled=True
        ).astype(jnp.float32),
        lax.psum_scatter(
            summed[7].astype(jnp.bfloat16), "fsdp", scatter_dimension=0, tiled=True
        ).astype(jnp.float32),
        lax.psum_scatter(
            summed[8].astype(jnp.bfloat16), "fsdp", scatter_dimension=0, tiled=True
        ).astype(jnp.float32),
        lax.psum_scatter(
            summed[9].astype(jnp.bfloat16), "fsdp", scatter_dimension=0, tiled=True
        ).astype(jnp.float32),
    )
    totals = (
        lax.psum(summed[0].astype(jnp.bfloat16), ("dp", "ctx")).astype(jnp.float32),
        lax.psum(summed[1].astype(jnp.bfloat16), ("dp", "ctx")).astype(jnp.float32),
        lax.psum(summed[2].astype(jnp.bfloat16), ("dp", "ctx")).astype(jnp.float32),
        lax.psum(summed[3].astype(jnp.bfloat16), ("dp", "ctx")).astype(jnp.float32),
        lax.psum(summed[4].astype(jnp.bfloat16), ("dp", "ctx")).astype(jnp.float32),
        lax.psum(summed[5].astype(jnp.bfloat16), ("dp", "ctx")).astype(jnp.float32),
        lax.psum(summed[6].astype(jnp.bfloat16), ("dp", "ctx")).astype(jnp.float32),
        lax.psum(summed[7].astype(jnp.bfloat16), ("dp", "ctx")).astype(jnp.float32),
        lax.psum(summed[8].astype(jnp.bfloat16), ("dp", "ctx")).astype(jnp.float32),
        lax.psum(summed[9].astype(jnp.bfloat16), ("dp", "ctx")).astype(jnp.float32),
    )
    stacked_out = jnp.stack(results)[None]
    stacked_back = jnp.stack(backs)[None]
    return (
        stacked_out,
        stacked_back,
        totals[0],
        totals[1],
        totals[2],
        totals[3],
        totals[4],
        totals[5],
        totals[6],
        totals[7],
        totals[8],
        totals[9],
    )


def solution(mesh):
    in_specs = (
        P(("dp", "fsdp"), None, "ctx", None),
        P(("dp", "fsdp"), None, "ctx", None),
        P(("dp", "fsdp"), None),
        P(("dp", "fsdp"), None, None),
        P("fsdp"),
        P("fsdp"),
        P("fsdp", None),
        P("fsdp"),
        P("fsdp", None),
        P("fsdp"),
        P("fsdp", None),
        P("fsdp"),
        P("fsdp", None),
        P("fsdp"),
    )
    out_specs = (
        P(("dp", "fsdp"), None, "ctx", None),
        P(("dp", "fsdp"), None, "ctx", None),
        P("fsdp"),
        P("fsdp"),
        P("fsdp", None),
        P("fsdp"),
        P("fsdp", None),
        P("fsdp"),
        P("fsdp", None),
        P("fsdp"),
        P("fsdp", None),
        P("fsdp"),
    )
    return jax.shard_map(body, mesh=mesh, in_specs=in_specs, out_specs=out_specs, check_vma=False)
```

profile of v0, /device:TPU:0, one launch (start us, length us, event | category | flops | bytes accessed | tf_op | source)
XLA Modules:
  0.0 3160.4 jit_solution(15819114740749781028)
XLA Ops:
  34.9 205.6 %all-gather.14.cloned.1.call-done = bf16[2048,6144]{1,0:T(8,128)(2,1)} async-done(((bf16[512,6144]{1,0:T(8,128)(2,1)}), bf16[2048,6144]{1,0:T(8,128)(2,1)}) %all-gather.14.cloned.1.call-update) | async-done | bytes 25165840 | tf_op jit(solution)/shard_map/all_gather | solution.py:249
  306.2 23.8 all-gather.20.cloned.1.call-done
  358.4 53.9 %all-gather.16.cloned.1.call-done = bf16[1024,2048]{1,0:T(8,128)(2,1)} async-done(((bf16[256,2048]{1,0:T(8,128)(2,1)}), bf16[1024,2048]{1,0:T(8,128)(2,1)}) %all-gather.16.cloned.1.call-update) | async-done | bytes 4194320 | tf_op jit(solution)/shard_map/all_gather | solution.py:84
  423.7 70.0 %all-gather.26.cloned.1.call-done = bf16[1024,2048]{1,0:T(8,128)(2,1)} async-done(((bf16[256,2048]{1,0:T(8,128)(2,1)}), bf16[1024,2048]{1,0:T(8,128)(2,1)}) %all-gather.26.cloned.1.call-update) | async-done | bytes 4194320 | tf_op jit(solution)/shard_map/all_gather | solution.py:84
  498.9 75.3 %all-gather.18.cloned.1.call-done = bf16[1024,2048]{0,1:T(8,128)(2,1)} async-done(((bf16[256,2048]{0,1:T(8,128)(2,1)}), bf16[1024,2048]{0,1:T(8,128)(2,1)}) %all-gather.18.cloned.1.call-update) | async-done | bytes 4194320 | tf_op jit(solution)/shard_map/all_gather | solution.py:83
  586.8 68.1 %all-gather.28.cloned.1.call-done = bf16[1024,2048]{0,1:T(8,128)(2,1)} async-done(((bf16[256,2048]{0,1:T(8,128)(2,1)}), bf16[1024,2048]{0,1:T(8,128)(2,1)}) %all-gather.28.cloned.1.call-update) | async-done | bytes 4194320 | tf_op jit(solution)/shard_map/all_gather | solution.py:83
  724.0 18.3 multiply_reduce_fusion.6
  742.4 26.8 multiply_convert_fusion.7
  832.5 18.6 multiply_reduce_fusion.2
  851.1 27.0 multiply_convert_fusion.3
  1014.6 31.2 reduce-scatter.15.cloned.1.call-done
  1045.9 20.5 fusion.190
  1066.4 59.6 %reduce-scatter.19.cloned.1.call-done = bf16[256,2048]{0,1:T(8,128)(2,1)} async-done(((bf16[1024,2048]{0,1:T(8,128)(2,1)}), bf16[256,2048]{0,1:T(8,128)(2,1)}) %reduce-scatter.19.cloned.1.call-update) | async-done | bytes 1048592 | tf_op jit(solution)/shard_map/reduce_scatter | solution.py:189
  1126.0 32.0 %add_convert_fusion.2 = bf16[2048,6144]{1,0:T(8,128)(2,1)} fusion(f32[2048,6144]{1,0:T(8,128)} %fusion.190, bf16[256,2048]{0,1:T(8,128)(2,1)} %reduce-scatter.19.cloned.1.call-done, bf16[256,2048]{0,1:T(8,128)(2,1)} %bitcast.429, bf16[256,2048]{0,1:T(8,128)(2,1)S(1)} %bitcast.426, f32[256]{0:T(256)S(1)} %copy-done.110, f32[256]{0:T(256)S(1)} %copy-done.107, ...), kind=kOutput, calls=%fused_computation.2 | convolution fusion | flops 6480199680 | bytes 79710208 | tf_op jit(solution)/shard_map/dot_general | solution.py:13
  1167.1 258.5 %all-gather.22.cloned.1.call-done = bf16[2048,8192]{1,0:T(8,128)(2,1)} async-done(((bf16[512,8192]{1,0:T(8,128)(2,1)}), bf16[2048,8192]{1,0:T(8,128)(2,1)}) %all-gather.22.cloned.1.call-update) | async-done | bytes 33554448 | tf_op jit(solution)/shard_map/all_gather | solution.py:253
  1425.7 21.7 convolution_add_fusion.1
  1447.3 19.0 convolution_add_fusion
  1466.3 258.3 %all-gather.24.cloned.1.call-done = bf16[8192,2048]{1,0:T(8,128)(2,1)} async-done(((bf16[2048,2048]{1,0:T(8,128)(2,1)}), bf16[8192,2048]{1,0:T(8,128)(2,1)}) %all-gather.24.cloned.1.call-update) | async-done | bytes 33554448 | tf_op jit(solution)/shard_map/all_gather | solution.py:255
  1724.6 21.7 convert_reduce_fusion.1
  1746.4 22.1 convert_reduce_fusion
  1768.5 27.0 fusion.207
  1795.5 37.4 %add_convert_fusion.1 = bf16[2048,8192]{1,0:T(8,128)(2,1)} fusion(f32[2048,8192]{1,0:T(8,128)} %fusion.207, bf16[256,8192]{1,0:T(8,128)(2,1)} %get-tuple-element.162, f32[256]{0:T(256)S(1)} %copy-done.110, f32[256]{0:T(256)S(1)} %copy-done.107, f32[2048]{0:T(1024)S(1)} %bitcast.481, f32[2048]{0:T(1024)S(1)} %bitcast.469, ...), kind=kOutput, calls=%fused_computation.1 | convolution fusion | flops 8626634752 | bytes 105924608 | tf_op jit(solution)/shard_map/dot_general | solution.py:13
  1833.0 30.1 fusion.192
  1863.0 39.8 %add_convert_fusion = bf16[8192,2048]{1,0:T(8,128)(2,1)} fusion(f32[8192,2048]{1,0:T(8,128)} %fusion.192, f32[256]{0:T(256)S(1)} %copy-done.154, bf16[1,2,256,2048]{3,2,1,0:T(8,128)(2,1)} %param.15, f32[256,8192]{1,0:T(8,128)} %convolution_add_fusion), kind=kOutput, calls=%fused_computation | convolution fusion | flops 8643936256 | bytes 110101504 | tf_op jit(solution)/shard_map/dot_general | solution.py:13
  1936.4 20.3 fusion.77
  1956.7 20.9 fusion.76
  1980.3 59.7 %reduce-scatter.21.cloned.1.call-done = bf16[512,6144]{1,0:T(8,128)(2,1)} async-done(((bf16[2048,6144]{1,0:T(8,128)(2,1)}), bf16[512,6144]{1,0:T(8,128)(2,1)}) %reduce-scatter.21.cloned.1.call-update) | async-done | bytes 6291472 | tf_op jit(solution)/shard_map/reduce_scatter | solution.py:275
  2040.0 291.6 %reduce-scatter.25.cloned.1.call-done = bf16[512,8192]{1,0:T(8,128)(2,1)} async-done(((bf16[2048,8192]{1,0:T(8,128)(2,1)}), bf16[512,8192]{1,0:T(8,128)(2,1)}) %reduce-scatter.25.cloned.1.call-update) | async-done | bytes 8388624
  2331.6 291.9 %reduce-scatter.27.cloned.1.call-done = bf16[2048,2048]{1,0:T(8,128)(2,1)} async-done(((bf16[8192,2048]{1,0:T(8,128)(2,1)}), bf16[2048,2048]{1,0:T(8,128)(2,1)}) %reduce-scatter.27.cloned.1.call-update) | async-done | bytes 8388624
  2670.4 18.7 fusion.94
  2711.4 29.8 all-reduce.7
  2746.6 373.5 %all-reduce.12.cloned.1.call-done = (bf16[512,6144]{1,0:T(8,128)(2,1)}, bf16[512,2048]{1,0:T(8,128)(2,1)}, bf16[512,8192]{1,0:T(8,128)(2,1)}, bf16[2048,2048]{1,0:T(8,128)(2,1)}) async-done(((bf16[512,6144]{1,0:T(8,128)(2,1)}, bf16[512,2048]{1,0:T(8,128)(2,1)}, bf16[512,8192]{1,0:T(8,128)(2,1)}, bf16[2048,2048]{1,0:T(8,128)(2,1)}), (bf16[512,6144]{1,0:T(8,128)(2,1)}, bf16[512,2048]{1,0:T(8,128)(2,1)}, ...) | async-done | bytes 25165840 | tf_op jit(solution)/shard_map/psum | solution.py:303
  (635 shorter events, 568.4 us)
Async XLA Ops:
  7.2 233.2 %all-gather.14.cloned.1.call-start = ((), (), s32[]{:S(2)}) async-start(), calls=%async_computation.8 | async-start | bytes 31457280 | tf_op jit(solution)/shard_map/all_gather | solution.py:249
  8.0 322.0 %all-gather.20.cloned.1.call-start = ((), (), s32[]{:S(2)}) async-start(), calls=%async_computation.11 | async-start | bytes 10485760 | tf_op jit(solution)/shard_map/all_gather | solution.py:251
  8.7 403.6 %all-gather.16.cloned.1.call-start = ((), (), s32[]{:S(2)}) async-start(), calls=%async_computation.9 | async-start | bytes 5242880 | tf_op jit(solution)/shard_map/all_gather | solution.py:84
  18.3 237.9 %copy-start.39 = (f32[4,1,512]{2,1,0:T(1,128)}, f32[4,1,512]{2,1,0:T(1,128)S(1)}, u32[]{:S(2)}) copy-start(f32[4,1,512]{2,1,0:T(1,128)S(1)} %convert_element_type.392) | copy-start | bytes 24580
  26.4 229.8 %copy-start.42 = (f32[4,1,512]{2,1,0:T(1,128)}, f32[4,1,512]{2,1,0:T(1,128)S(1)}, u32[]{:S(2)}) copy-start(f32[4,1,512]{2,1,0:T(1,128)S(1)} %convert_element_type.393) | copy-start | bytes 24580
  34.2 218.1 %copy-start.80 = (f32[256]{0:T(256)}, f32[256]{0:T(256)S(1)}, u32[]{:S(2)}) copy-start(f32[256]{0:T(256)S(1)} %get-tuple-element.164) | copy-start | bytes 3076
  34.2 222.0 %copy-start.106 = (f32[256]{0:T(256)}, f32[256]{0:T(256)S(1)}, u32[]{:S(2)}) copy-start(f32[256]{0:T(256)S(1)} %get-tuple-element.163) | copy-start | bytes 3076
  34.9 217.4 %copy-start.99 = (f32[256]{0:T(256)}, f32[256]{0:T(256)S(1)}, u32[]{:S(2)}) copy-start(f32[256]{0:T(256)S(1)} %add_rsqrt_fusion.1) | copy-start | bytes 3076
  256.1 237.5 %all-gather.26.cloned.1.call-start = ((), (), s32[]{:S(2)}) async-start(), calls=%async_computation.14 | async-start | bytes 5242880 | tf_op jit(solution)/shard_map/all_gather | solution.py:84
  271.9 302.2 %all-gather.18.cloned.1.call-start = ((), (), s32[]{:S(2)}) async-start(), calls=%async_computation.10 | async-start | bytes 5242880 | tf_op jit(solution)/shard_map/all_gather | solution.py:83
  286.2 368.8 %all-gather.28.cloned.1.call-start = ((), (), s32[]{:S(2)}) async-start(), calls=%async_computation.15 | async-start | bytes 5242880 | tf_op jit(solution)/shard_map/all_gather | solution.py:83
  287.5 42.4 %copy-start.155 = (f32[256]{0:T(256)}, f32[256]{0:T(256)S(1)}, u32[]{:S(2)}) copy-start(f32[256]{0:T(256)S(1)} %compare_convert_fusion.1) | copy-start | bytes 3076
  289.0 49.6 %copy-start.153 = (f32[256]{0:T(256)}, f32[256]{0:T(256)S(1)}, u32[]{:S(2)}) copy-start(f32[256]{0:T(256)S(1)} %compare_convert_fusion) | copy-start | bytes 3076
  304.6 696.4 %reduce-scatter.13.cloned.1.call-start = ((), (), s32[]{:S(2)}) async-start(), calls=%async_computation.16 | async-start | bytes 5242880 | tf_op jit(solution)/shard_map/reduce_scatter | solution.py:186
  577.9 95.7 %copy-start.27 = (bf16[1024,512]{0,1:T(8,128)(2,1)}, bf16[1024,512]{0,1:T(8,128)(2,1)S(1)}, u32[]{:S(2)}) copy-start(bf16[1024,512]{0,1:T(8,128)(2,1)S(1)} %get-tuple-element.72) | copy-start | bytes 3145732
  577.9 101.5 %copy-start.31 = (bf16[1024,512]{0,1:T(8,128)(2,1)}, bf16[1024,512]{0,1:T(8,128)(2,1)S(1)}, u32[]{:S(2)}) copy-start(bf16[1024,512]{0,1:T(8,128)(2,1)S(1)} %get-tuple-element.74) | copy-start | bytes 3145732
  580.7 78.3 %copy-start.134 = (f32[8,256]{1,0:T(8,128)}, f32[8,256]{1,0:T(8,128)S(1)}, u32[]{:S(2)}) copy-start(f32[8,256]{1,0:T(8,128)S(1)} %get-tuple-element.153) | copy-start | bytes 24580
  782.4 222.5 %reduce-scatter.17.cloned.1.call-start = ((), (), s32[]{:S(2)}) async-start(), calls=%async_computation.18 | async-start | bytes 5242880 | tf_op jit(solution)/shard_map/reduce_scatter | solution.py:186
  891.2 154.7 %reduce-scatter.15.cloned.1.call-start = ((), (), s32[]{:S(2)}) async-start(), calls=%async_computation.17 | async-start | bytes 5242880 | tf_op jit(solution)/shard_map/reduce_scatter | solution.py:189
  910.7 215.3 %reduce-scatter.19.cloned.1.call-start = ((), (), s32[]{:S(2)}) async-start(), calls=%async_computation.19 | async-start | bytes 5242880 | tf_op jit(solution)/shard_map/reduce_scatter | solution.py:189
  930.5 495.1 %all-gather.22.cloned.1.call-start = ((), (), s32[]{:S(2)}) async-start(), calls=%async_computation.12 | async-start | bytes 41943040 | tf_op jit(solution)/shard_map/all_gather | solution.py:253
  931.3 793.4 %all-gather.24.cloned.1.call-start = ((), (), s32[]{:S(2)}) async-start(), calls=%async_computation.13 | async-start | bytes 41943040 | tf_op jit(solution)/shard_map/all_gather | solution.py:255
  931.9 1048.4 %reduce-scatter.23.cloned.1.call-start = ((), (), s32[]{:S(2)}) async-start(), calls=%async_computation.21 | async-start | bytes 10485760 | tf_op jit(solution)/shard_map/reduce_scatter | solution.py:281
  979.9 1060.1 %reduce-scatter.21.cloned.1.call-start = ((), (), s32[]{:S(2)}) async-start(), calls=%async_computation.20 | async-start | bytes 31457280 | tf_op jit(solution)/shard_map/reduce_scatter | solution.py:275
  1013.4 112.6 %copy-start.17 = (bf16[256,32,64]{0,2,1:T(8,128)(2,1)}, bf16[256,32,64]{0,2,1:T(8,128)(2,1)S(1)}, u32[]{:S(2)}) copy-start(bf16[256,32,64]{0,2,1:T(8,128)(2,1)S(1)} %pad_maximum_fusion.16) | copy-start | bytes 3145732
  1045.9 80.1 %copy-start.107 = (f32[256]{0:T(256)S(1)}, f32[256]{0:T(256)}, u32[]{:S(2)}) copy-start(f32[256]{0:T(256)} %copy-done.106) | copy-start | bytes 3076
  1045.9 80.1 %copy-start.110 = (f32[256]{0:T(256)S(1)}, f32[256]{0:T(256)}, u32[]{:S(2)}) copy-start(f32[256]{0:T(256)} %copy-done.109) | copy-start | bytes 3076
  1158.0 1173.6 %reduce-scatter.25.cloned.1.call-start = ((), (), s32[]{:S(2)}) async-start(), calls=%async_computation.22 | async-start | bytes 41943040
  1447.3 277.3 %copy-start.157 = (f32[256]{0:T(256)S(1)}, f32[256]{0:T(256)}, u32[]{:S(2)}) copy-start(f32[256]{0:T(256)} %copy-done.155) | copy-start | bytes 3076
  1832.9 790.5 %reduce-scatter.27.cloned.1.call-start = ((), (), s32[]{:S(2)}) async-start(), calls=%async_computation.23 | async-start | bytes 41943040
  1902.9 1217.2 %all-reduce.12.cloned.1.call-start = ((), (), s32[]{:S(2)}) async-start(), calls=%async_computation.24 | async-start | bytes 50331648 | tf_op jit(solution)/shard_map/psum | solution.py:303
  2742.4 410.4 %copy-start.158 = (f32[512]{0:T(512)}, f32[512]{0:T(512)S(1)}, u32[]{:S(2)}) copy-start(f32[512]{0:T(512)S(1)} %convert_element_type.381) | copy-start | bytes 6148
  (179 other events, 1623.7 us)
Sparse Core Ops, SparseCore 0:
  9.9 230.4 all-gather.13
  242.3 87.6 all-gather.19
  331.5 80.7 all-gather.15
  414.3 79.2 all-gather.25
  495.0 79.0 all-gather.17
  576.2 78.7 all-gather.27
  782.5 74.9 reduce-scatter.12
  891.3 74.8 reduce-scatter.16
  968.6 77.2 reduce-scatter.14
  1048.7 77.2 reduce-scatter.18
  1127.8 297.7 all-gather.21
  1427.4 297.2 all-gather.23
  1728.2 86.4 reduce-scatter.22
  1818.0 221.9 reduce-scatter.20
  2042.9 288.6 reduce-scatter.24
  2334.8 288.6 reduce-scatter.26
  2626.2 493.8 all-reduce.11
where the time goes:
time: 3170 us; the launch traced here: 3160 us
  waiting for transfers between devices  2120 us (67%)
  matrix products  665 us (21%)
  other arithmetic  161 us (5%)
  local copies, waits for them, and re-layouts  95.3 us (3%)
  blocking collectives  93.9 us (3%)
    unnamed x19, waiting for transfers between devices  586 us
    psum x1, waiting for transfers between devices, body(): lax.psum(summed[2].astype(jnp.bfloat16), ('dp', 'ctx')).astype(jnp.float32)  374 us
    all_gather x1, waiting for transfers between devices, body(): lax.all_gather(w_up, 'fsdp', axis=0, tiled=True)  259 us
    all_gather x1, waiting for transfers between devices, body(): lax.all_gather(w_down, 'fsdp', axis=0, tiled=True)  258 us
    dot_general x8, matrix products, contract_rows(): lax.dot_general(left, right, (((0,), (0,)), ((), ())), preferred_element_...  206 us
    all_gather x1, waiting for transfers between devices, body(): lax.all_gather(w_qkv, 'fsdp', axis=0, tiled=True)  206 us
    all_gather x2, waiting for transfers between devices, layer_step(): lax.all_gather(keyed, 'ctx', axis=0, tiled=True)  143 us
    all_gather x2, waiting for transfers between devices, layer_step(): lax.all_gather(valued, 'ctx', axis=0, tiled=True)  124 us
  transfers between devices with their start and end apart: 17, of which 14 were waited for; matrix products, arithmetic and copies ran while one was open for 24% of the time, Pallas kernels for 0%

commit v1 on v0

--- a/solution.py
+++ b/solution.py
@@ -300,7 +300,9 @@
     totals = (
         lax.psum(summed[0].astype(jnp.bfloat16), ("dp", "ctx")).astype(jnp.float32),
         lax.psum(summed[1].astype(jnp.bfloat16), ("dp", "ctx")).astype(jnp.float32),
-        lax.psum(summed[2].astype(jnp.bfloat16), ("dp", "ctx")).astype(jnp.float32),
+        jnp.sum(
+            lax.all_gather(summed[2].astype(jnp.bfloat16), axis_name=("dp", "ctx")), axis=0
+        ).astype(jnp.float32),
         lax.psum(summed[3].astype(jnp.bfloat16), ("dp", "ctx")).astype(jnp.float32),
         lax.psum(summed[4].astype(jnp.bfloat16), ("dp", "ctx")).astype(jnp.float32),
         lax.psum(summed[5].astype(jnp.bfloat16), ("dp", "ctx")).astype(jnp.float32),

time: 3170 us -> 3320 us (1.047)
  waiting for transfers between devices: 2120 us -> 2250 us
  other arithmetic: 161 us -> 195 us
    all_gather x0 -> x1, waiting for transfers between devices: none -> 396 us  [body(): lax.all_gather(summed[2].astype(jnp.bfloat16), axis_name=('dp', 'ctx'))]
    all_gather x1, waiting for transfers between devices: 259 us -> 0.02 us  [body(): lax.all_gather(w_up, 'fsdp', axis=0, tiled=True)]
    psum x1, waiting for transfers between devices: 374 us -> 178 us  [body(): lax.psum(summed[4].astype(jnp.bfloat16), ('dp', 'ctx')).astype(jnp.float32)]
    reduce_scatter x1, waiting for transfers between devices: 59.7 us -> 225 us  [body(): lax.psum_scatter(summed[2].astype(jnp.bfloat16), 'fsdp', scatter_dimensio...]
    reduce_scatter x1, waiting for transfers between devices: 0.01 us -> 62.7 us  [body(): lax.psum_scatter(summed[4].astype(jnp.bfloat16), 'fsdp', scatter_dimensio...]
    all_gather x1, waiting for transfers between devices: 258 us -> 219 us  [body(): lax.all_gather(w_down, 'fsdp', axis=0, tiled=True)]
    unnamed x19 -> x20, waiting for transfers between devices: 586 us -> 586 us
  transfers between devices with their start and end apart: 17 -> 18, of which waited for: 14 -> 15; matrix products, arithmetic and copies ran while one was open for 24% -> 27% of each run, Pallas kernels for 0% -> 0%
where the time goes in v1:
time: 3320 us; the launch traced here: 3310 us
  waiting for transfers between devices  2250 us (68%)
  matrix products  657 us (20%)
  other arithmetic  195 us (6%)
  local copies, waits for them, and re-layouts  94.3 us (3%)
  blocking collectives  94.3 us (3%)
    unnamed x20, waiting for transfers between devices  586 us
    all_gather x1, waiting for transfers between devices, body(): lax.all_gather(summed[2].astype(jnp.bfloat16), axis_name=('dp', 'ctx'))  396 us
    reduce_scatter x1, waiting for transfers between devices, body(): lax.psum_scatter(summed[2].astype(jnp.bfloat16), 'fsdp', scatter_dimensio...  225 us
    all_gather x1, waiting for transfers between devices, body(): lax.all_gather(w_down, 'fsdp', axis=0, tiled=True)  219 us
    all_gather x1, waiting for transfers between devices, body(): lax.all_gather(w_qkv, 'fsdp', axis=0, tiled=True)  206 us
    dot_general x8, matrix products, contract_rows(): lax.dot_general(left, right, (((0,), (0,)), ((), ())), preferred_element_...  198 us
    psum x1, waiting for transfers between devices, body(): lax.psum(summed[4].astype(jnp.bfloat16), ('dp', 'ctx')).astype(jnp.float32)  178 us
    all_gather x2, waiting for transfers between devices, layer_step(): lax.all_gather(keyed, 'ctx', axis=0, tiled=True)  139 us
  transfers between devices with their start and end apart: 18, of which 15 were waited for; matrix products, arithmetic and copies ran while one was open for 27% of the time, Pallas kernels for 0%

profile of v1, /device:TPU:0, one launch (start us, length us, event | category | flops | bytes accessed | tf_op | source)
XLA Modules:
  0.0 3313.4 jit_solution(4452613626124083830)
XLA Ops:
  34.8 205.6 %all-gather.16.cloned.1.call-done = bf16[2048,6144]{1,0:T(8,128)(2,1)} async-done(((bf16[512,6144]{1,0:T(8,128)(2,1)}), bf16[2048,6144]{1,0:T(8,128)(2,1)}) %all-gather.16.cloned.1.call-update) | async-done | bytes 25165840 | tf_op jit(solution)/shard_map/all_gather | solution.py:249
  305.7 24.2 all-gather.22.cloned.1.call-done
  358.3 54.5 %all-gather.28.cloned.1.call-done = bf16[1024,2048]{1,0:T(8,128)(2,1)} async-done(((bf16[256,2048]{1,0:T(8,128)(2,1)}), bf16[1024,2048]{1,0:T(8,128)(2,1)}) %all-gather.28.cloned.1.call-update) | async-done | bytes 4194320 | tf_op jit(solution)/shard_map/all_gather | solution.py:84
  424.1 69.5 %all-gather.18.cloned.1.call-done = bf16[1024,2048]{1,0:T(8,128)(2,1)} async-done(((bf16[256,2048]{1,0:T(8,128)(2,1)}), bf16[1024,2048]{1,0:T(8,128)(2,1)}) %all-gather.18.cloned.1.call-update) | async-done | bytes 4194320 | tf_op jit(solution)/shard_map/all_gather | solution.py:84
  504.7 70.0 %all-gather.30.cloned.1.call-done = bf16[1024,2048]{0,1:T(8,128)(2,1)} async-done(((bf16[256,2048]{0,1:T(8,128)(2,1)}), bf16[1024,2048]{0,1:T(8,128)(2,1)}) %all-gather.30.cloned.1.call-update) | async-done | bytes 4194320 | tf_op jit(solution)/shard_map/all_gather | solution.py:83
  586.4 69.1 %all-gather.20.cloned.1.call-done = bf16[1024,2048]{0,1:T(8,128)(2,1)} async-done(((bf16[256,2048]{0,1:T(8,128)(2,1)}), bf16[1024,2048]{0,1:T(8,128)(2,1)}) %all-gather.20.cloned.1.call-update) | async-done | bytes 4194320 | tf_op jit(solution)/shard_map/all_gather | solution.py:83
  756.1 18.4 multiply_reduce_fusion.2
  774.5 29.8 multiply_convert_fusion.3
  828.5 21.0 multiply_reduce_fusion.6
  849.5 26.6 multiply_convert_fusion.7
  1032.7 219.3 %all-gather.26.cloned.1.call-done = bf16[8192,2048]{1,0:T(8,128)(2,1)} async-done(((bf16[2048,2048]{1,0:T(8,128)(2,1)}), bf16[8192,2048]{1,0:T(8,128)(2,1)}) %all-gather.26.cloned.1.call-update) | async-done | bytes 33554448 | tf_op jit(solution)/shard_map/all_gather | solution.py:255
  1252.0 21.7 convert_reduce_fusion
  1273.7 21.9 convert_reduce_fusion.1
  1295.7 25.7 fusion.207
  1321.4 34.8 %add_convert_fusion.1 = bf16[2048,8192]{1,0:T(8,128)(2,1)} fusion(f32[2048,8192]{1,0:T(8,128)} %fusion.207, bf16[256,8192]{1,0:T(8,128)(2,1)} %get-tuple-element.161, f32[256]{0:T(256)S(1)} %copy-done.104, f32[256]{0:T(256)S(1)} %copy-done.102, f32[2048]{0:T(1024)S(1)} %bitcast.475, f32[2048]{0:T(1024)S(1)} %bitcast.465, ...), kind=kOutput, calls=%fused_computation.1 | convolution fusion | flops 8626634752 | bytes 105924608 | tf_op jit(solution)/shard_map/dot_general | solution.py:13
  1356.2 27.8 fusion.192
  1384.0 38.3 %add_convert_fusion = bf16[8192,2048]{1,0:T(8,128)(2,1)} fusion(f32[8192,2048]{1,0:T(8,128)} %fusion.192, f32[256]{0:T(256)S(1)} %copy-done.140, bf16[1,2,256,2048]{3,2,1,0:T(8,128)(2,1)} %param.15, f32[256,8192]{1,0:T(8,128)} %convolution_add_fusion), kind=kOutput, calls=%fused_computation | convolution fusion | flops 8643936256 | bytes 110101504 | tf_op jit(solution)/shard_map/dot_general | solution.py:13
  1459.4 30.8 reduce-scatter.15.cloned.1.call-done
  1490.2 20.7 fusion.190
  1510.9 59.5 %reduce-scatter.19.cloned.1.call-done = bf16[256,2048]{0,1:T(8,128)(2,1)} async-done(((bf16[1024,2048]{0,1:T(8,128)(2,1)}), bf16[256,2048]{0,1:T(8,128)(2,1)}) %reduce-scatter.19.cloned.1.call-update) | async-done | bytes 1048592 | tf_op jit(solution)/shard_map/reduce_scatter | solution.py:189
  1570.4 27.8 add_convert_fusion.2
  1598.2 62.7 %reduce-scatter.23.cloned.1.call-done = bf16[512,2048]{1,0:T(8,128)(2,1)} async-done(((bf16[2048,2048]{1,0:T(8,128)(2,1)}), bf16[512,2048]{1,0:T(8,128)(2,1)}) %reduce-scatter.23.cloned.1.call-update) | async-done | bytes 2097168 | tf_op jit(solution)/shard_map/reduce_scatter | solution.py:281
  1660.9 291.9 %reduce-scatter.25.cloned.1.call-done = bf16[512,8192]{1,0:T(8,128)(2,1)} async-done(((bf16[2048,8192]{1,0:T(8,128)(2,1)}), bf16[512,8192]{1,0:T(8,128)(2,1)}) %reduce-scatter.25.cloned.1.call-update) | async-done | bytes 8388624
  1952.8 291.6 %reduce-scatter.27.cloned.1.call-done = bf16[2048,2048]{1,0:T(8,128)(2,1)} async-done(((bf16[8192,2048]{1,0:T(8,128)(2,1)}), bf16[2048,2048]{1,0:T(8,128)(2,1)}) %reduce-scatter.27.cloned.1.call-update) | async-done | bytes 8388624
  2244.5 225.1 %reduce-scatter.21.cloned.1.call-done = bf16[512,6144]{1,0:T(8,128)(2,1)} async-done(((bf16[2048,6144]{1,0:T(8,128)(2,1)}), bf16[512,6144]{1,0:T(8,128)(2,1)}) %reduce-scatter.21.cloned.1.call-update) | async-done | bytes 6291472 | tf_op jit(solution)/shard_map/reduce_scatter | solution.py:275
  2502.0 20.3 fusion.76
  2522.4 20.1 fusion.77
  2591.7 18.8 fusion.94
  2633.4 29.8 all-reduce.7
  2668.9 178.2 %all-reduce.12.cloned.1.call-done = (bf16[512,2048]{1,0:T(8,128)(2,1)}, bf16[512,8192]{1,0:T(8,128)(2,1)}, bf16[2048,2048]{1,0:T(8,128)(2,1)}) async-done(((bf16[512,2048]{1,0:T(8,128)(2,1)}, bf16[512,8192]{1,0:T(8,128)(2,1)}, bf16[2048,2048]{1,0:T(8,128)(2,1)}), (bf16[512,2048]{1,0:T(8,128)(2,1)}, bf16[512,8192]{1,0:T(8,128)(2,1)}, bf16[2048,2048]{1,0:T(8,128)(2,1)})) %all-reduce.12.cloned.1.call-update) | async-done | bytes 18874384 | tf_op jit(solution)/shard_map/psum | solution.py:307
  2880.5 395.5 %all-gather.32.cloned.1.call-done = bf16[4096,6144]{1,0:T(8,128)(2,1)} async-done(((bf16[512,6144]{1,0:T(8,128)(2,1)}), bf16[4096,6144]{1,0:T(8,128)(2,1)}) %all-gather.32.cloned.1.call-update) | async-done | bytes 50331664 | tf_op jit(solution)/shard_map/all_gather | solution.py:304
  3276.1 20.1 reduce_sum.346
  (596 shorter events, 622.9 us)
Async XLA Ops:
  7.2 233.2 %all-gather.16.cloned.1.call-start = ((), (), s32[]{:S(2)}) async-start(), calls=%async_computation.8 | async-start | bytes 31457280 | tf_op jit(solution)/shard_map/all_gather | solution.py:249
  8.0 321.9 %all-gather.22.cloned.1.call-start = ((), (), s32[]{:S(2)}) async-start(), calls=%async_computation.11 | async-start | bytes 10485760 | tf_op jit(solution)/shard_map/all_gather | solution.py:251
  8.7 404.1 %all-gather.28.cloned.1.call-start = ((), (), s32[]{:S(2)}) async-start(), calls=%async_computation.14 | async-start | bytes 5242880 | tf_op jit(solution)/shard_map/all_gather | solution.py:84
  26.5 229.6 %copy-start.39 = (f32[4,1,512]{2,1,0:T(1,128)}, f32[4,1,512]{2,1,0:T(1,128)S(1)}, u32[]{:S(2)}) copy-start(f32[4,1,512]{2,1,0:T(1,128)S(1)} %convert_element_type.395) | copy-start | bytes 24580
  33.7 222.5 %copy-start.37 = (f32[4,1,512]{2,1,0:T(1,128)}, f32[4,1,512]{2,1,0:T(1,128)S(1)}, u32[]{:S(2)}) copy-start(f32[4,1,512]{2,1,0:T(1,128)S(1)} %convert_element_type.394) | copy-start | bytes 24580
  34.0 218.1 %copy-start.101 = (f32[256]{0:T(256)}, f32[256]{0:T(256)S(1)}, u32[]{:S(2)}) copy-start(f32[256]{0:T(256)S(1)} %get-tuple-element.162) | copy-start | bytes 3076
  34.0 222.1 %copy-start.78 = (f32[256]{0:T(256)}, f32[256]{0:T(256)S(1)}, u32[]{:S(2)}) copy-start(f32[256]{0:T(256)S(1)} %get-tuple-element.163) | copy-start | bytes 3076
  34.7 217.4 %copy-start.103 = (f32[256]{0:T(256)}, f32[256]{0:T(256)S(1)}, u32[]{:S(2)}) copy-start(f32[256]{0:T(256)S(1)} %add_rsqrt_fusion) | copy-start | bytes 3076
  256.0 237.5 %all-gather.18.cloned.1.call-start = ((), (), s32[]{:S(2)}) async-start(), calls=%async_computation.9 | async-start | bytes 5242880 | tf_op jit(solution)/shard_map/all_gather | solution.py:84
  271.8 302.9 %all-gather.30.cloned.1.call-start = ((), (), s32[]{:S(2)}) async-start(), calls=%async_computation.15 | async-start | bytes 5242880 | tf_op jit(solution)/shard_map/all_gather | solution.py:83
  285.9 369.6 %all-gather.20.cloned.1.call-start = ((), (), s32[]{:S(2)}) async-start(), calls=%async_computation.10 | async-start | bytes 5242880 | tf_op jit(solution)/shard_map/all_gather | solution.py:83
  299.6 697.6 %all-gather.24.cloned.1.call-start = ((), (), s32[]{:S(2)}) async-start(), calls=%async_computation.12 | async-start | bytes 41943040 | tf_op jit(solution)/shard_map/all_gather | solution.py:253
  300.3 951.7 %all-gather.26.cloned.1.call-start = ((), (), s32[]{:S(2)}) async-start(), calls=%async_computation.13 | async-start | bytes 41943040 | tf_op jit(solution)/shard_map/all_gather | solution.py:255
  301.1 1143.2 %reduce-scatter.17.cloned.1.call-start = ((), (), s32[]{:S(2)}) async-start(), calls=%async_computation.18 | async-start | bytes 5242880 | tf_op jit(solution)/shard_map/reduce_scatter | solution.py:186
  304.3 34.1 %copy-start.141 = (f32[256]{0:T(256)}, f32[256]{0:T(256)S(1)}, u32[]{:S(2)}) copy-start(f32[256]{0:T(256)S(1)} %compare_convert_fusion.1) | copy-start | bytes 3076
  358.3 301.1 %copy-start.53 = (bf16[256,512]{0,1:T(8,128)(2,1)}, bf16[256,512]{0,1:T(8,128)(2,1)S(1)}, u32[]{:S(2)}) copy-start(bf16[256,512]{0,1:T(8,128)(2,1)S(1)} %get-tuple-element.112) | copy-start | bytes 786436
  578.4 84.9 %copy-start.29 = (bf16[1024,512]{0,1:T(8,128)(2,1)}, bf16[1024,512]{0,1:T(8,128)(2,1)S(1)}, u32[]{:S(2)}) copy-start(bf16[1024,512]{0,1:T(8,128)(2,1)S(1)} %get-tuple-element.80) | copy-start | bytes 3145732
  578.4 93.1 %copy-start.22 = (bf16[1024,512]{0,1:T(8,128)(2,1)}, bf16[1024,512]{0,1:T(8,128)(2,1)S(1)}, u32[]{:S(2)}) copy-start(bf16[1024,512]{0,1:T(8,128)(2,1)S(1)} %get-tuple-element.81) | copy-start | bytes 3145732
  817.5 631.4 %reduce-scatter.13.cloned.1.call-start = ((), (), s32[]{:S(2)}) async-start(), calls=%async_computation.16 | async-start | bytes 5242880 | tf_op jit(solution)/shard_map/reduce_scatter | solution.py:186
  889.2 601.0 %reduce-scatter.15.cloned.1.call-start = ((), (), s32[]{:S(2)}) async-start(), calls=%async_computation.17 | async-start | bytes 5242880 | tf_op jit(solution)/shard_map/reduce_scatter | solution.py:189
  908.8 661.5 %reduce-scatter.19.cloned.1.call-start = ((), (), s32[]{:S(2)}) async-start(), calls=%async_computation.19 | async-start | bytes 5242880 | tf_op jit(solution)/shard_map/reduce_scatter | solution.py:189
  949.9 711.1 %reduce-scatter.23.cloned.1.call-start = ((), (), s32[]{:S(2)}) async-start(), calls=%async_computation.21 | async-start | bytes 10485760 | tf_op jit(solution)/shard_map/reduce_scatter | solution.py:281
  996.6 956.1 %reduce-scatter.25.cloned.1.call-start = ((), (), s32[]{:S(2)}) async-start(), calls=%async_computation.23 | async-start | bytes 41943040
  1356.1 888.3 %reduce-scatter.27.cloned.1.call-start = ((), (), s32[]{:S(2)}) async-start(), calls=%async_computation.24 | async-start | bytes 41943040
  1422.4 1047.2 %reduce-scatter.21.cloned.1.call-start = ((), (), s32[]{:S(2)}) async-start(), calls=%async_computation.20 | async-start | bytes 31457280 | tf_op jit(solution)/shard_map/reduce_scatter | solution.py:275
  1598.2 1248.9 %all-reduce.12.cloned.1.call-start = ((), (), s32[]{:S(2)}) async-start(), calls=%async_computation.25 | async-start | bytes 37748736 | tf_op jit(solution)/shard_map/psum | solution.py:307
  2244.4 225.2 %copy-start.151 = (bf16[512]{0:T(512)(128)(2,1)S(1)}, bf16[512]{0:T(512)(128)(2,1)}, u32[]{:S(2)}) copy-start(bf16[512]{0:T(512)(128)(2,1)} %param.23) | copy-start | bytes 3076
  2244.4 233.1 %copy-start.152 = (bf16[512]{0:T(512)(128)(2,1)S(1)}, bf16[512]{0:T(512)(128)(2,1)}, u32[]{:S(2)}) copy-start(bf16[512]{0:T(512)(128)(2,1)} %param.27) | copy-start | bytes 3076
  2244.4 240.4 %copy-start.153 = (u32[32]{0:T(128)S(1)}, u32[32]{0:T(128)}, u32[]{:S(2)}) copy-start(u32[32]{0:T(128)} %constant.66) | copy-start | bytes 388
  2244.4 242.9 %copy-start.90 = (bf16[8,64,256]{2,1,0:T(8,128)(2,1)S(1)}, bf16[8,64,256]{2,1,0:T(8,128)(2,1)}, u32[]{:S(2)}) copy-start(bf16[8,64,256]{2,1,0:T(8,128)(2,1)} %copy-done.89) | copy-start | bytes 786436
  2244.4 1031.7 %all-gather.32.cloned.1.call-start = ((), (), s32[]{:S(2)}) async-start(), calls=%async_computation.22 | async-start | bytes 56623104 | tf_op jit(solution)/shard_map/all_gather | solution.py:304
  2665.0 640.5 %copy-start.144 = (f32[512]{0:T(512)}, f32[512]{0:T(512)S(1)}, u32[]{:S(2)}) copy-start(f32[512]{0:T(512)S(1)} %convert_element_type.383) | copy-start | bytes 6148
  (160 other events, 1357.8 us)
Sparse Core Ops, SparseCore 0:
  9.9 230.4 all-gather.15
  242.2 87.6 all-gather.21
  332.0 80.7 all-gather.27
  414.3 79.2 all-gather.17
  495.6 79.0 all-gather.29
  576.7 78.7 all-gather.19
  657.3 295.5 all-gather.23
  954.7 297.2 all-gather.25
  1254.3 76.7 reduce-scatter.16
  1333.3 77.2 reduce-scatter.12
  1412.9 77.2 reduce-scatter.14
  1493.0 77.2 reduce-scatter.18
  1574.0 86.8 reduce-scatter.22
  1664.1 288.6 reduce-scatter.24
  1955.7 288.6 reduce-scatter.26
  2247.7 221.8 reduce-scatter.20
  2472.2 374.8 all-reduce.11
  2848.5 427.5 all-gather.31
